TPU v7x, 32 devices: a whole 2x2x4 slice. The times are simulated.
32 devices in a mesh: dp: 8 (over z, y), expert: 4 (over x, core).
Axes of the slice: x: 2, y: 2, z: 4, core: 2. Of those that a mesh axis runs over, the one named last changes fastest.
Arguments:
- tokens: bfloat16 [512, 2048], P(('dp', 'expert')), may hold values from -6 to 6
- expert_ids: int32 [512, 8], P(('dp', 'expert')), may hold values from 0 to 15, as said below
- route_weight: float32 [512, 8], P(('dp', 'expert')), may hold values from 0.03 to 0.6
- out_grad: bfloat16 [512, 2048], P(('dp', 'expert')), may hold values from -6 to 6
- gate_weight: bfloat16 [32, 2048, 384], P(('dp', 'expert')), may hold values from -0.125 to 0.125
- up_weight: bfloat16 [32, 2048, 384], P(('dp', 'expert')), may hold values from -0.125 to 0.125
- down_weight: bfloat16 [32, 384, 2048], P(('dp', 'expert')), may hold values from -0.21875 to 0.21875
Outputs:
- layer_out: bfloat16 [512, 2048], P(('dp', 'expert'))
- token_grad: bfloat16 [512, 2048], P(('dp', 'expert'))
- route_grad: float32 [512, 8], P(('dp', 'expert'))
- gate_grad: bfloat16 [32, 2048, 384], P(('dp', 'expert'))
- up_grad: bfloat16 [32, 2048, 384], P(('dp', 'expert'))
- down_grad: bfloat16 [32, 384, 2048], P(('dp', 'expert'))
Inputs may be any that keep to these rules, and one draw needn't show every extreme that they name: `expert_ids`: each row names 8 different experts. The rows of one device name no expert more than 16 times, and one expert is named exactly 16 times by the rows of every device.
All inputs are finite; a program needn't handle non-finite values.
Results may differ from a plain program's by a relative error of at most 0.0071.
Values may be sent and summed in bfloat16 or wider, within the bound.
A program may use at most 128 MiB of HBM per device.

v0:
```python
import jax
import jax.numpy as jnp
from jax import lax
from jax.sharding import PartitionSpec as P


def from_partner(shard, axis, apart):
    return lax.ppermute(shard, axis, [(i, i ^ 1 << apart) for i in range(lax.axis_size(axis))])


def contract(left_op, right_op, left_dim, right_dim):
    return lax.dot_general(
        left_op,
        right_op,
        (((left_dim,), (right_dim,)), ((), ())),
        preferred_element_type=jnp.float32,
    )


def deliver(buffer, dp_size, ex_size, experts, capacity, backward):
    feat_width = buffer.shape[1]
    doubled = jnp.broadcast_to(
        buffer.reshape(experts, 1, capacity, feat_width), (experts, 2, capacity, feat_width)
    )
    doubled = doubled.reshape(dp_size, ex_size, capacity, feat_width)
    if backward:
        arrived = lax.all_to_all(
            lax.all_to_all(doubled, "dp", split_axis=0, concat_axis=0, tiled=True),
            "expert",
            split_axis=1,
            concat_axis=1,
            tiled=True,
        )
    else:
        arrived = lax.all_to_all(
            lax.all_to_all(doubled, "dp", split_axis=0, concat_axis=0, tiled=True),
            "expert",
            split_axis=1,
            concat_axis=1,
            tiled=True,
        )
    return arrived.reshape(-1, feat_width)


def bring_back(partials_in, dp_size, ex_size, experts, capacity, half_index, backward):
    feat_width = partials_in.shape[1]
    if backward:
        partner = from_partner(partials_in, "expert", 0)
    else:
        partner = from_partner(partials_in, "expert", 0)
    summed = (partials_in.astype(jnp.float32) + partner.astype(jnp.float32)).astype(jnp.bfloat16)
    summed = summed.reshape(dp_size, ex_size, capacity, feat_width)
    own_half = lax.dynamic_slice_in_dim(summed, half_index * (capacity // 2), capacity // 2, 2)
    if backward:
        returned = lax.all_to_all(
            lax.all_to_all(own_half, "dp", split_axis=0, concat_axis=0, tiled=True),
            "expert",
            split_axis=1,
            concat_axis=1,
            tiled=True,
        )
    else:
        returned = lax.all_to_all(
            lax.all_to_all(own_half, "dp", split_axis=0, concat_axis=0, tiled=True),
            "expert",
            split_axis=1,
            concat_axis=1,
            tiled=True,
        )
    merged = returned.reshape(experts, capacity, feat_width)
    return merged.reshape(experts * capacity, feat_width)


AXES = ("dp", "expert")


def dense_body(tokens, expert_ids, route_weight, out_grad, gate_weight, up_weight, down_weight):
    pieces = lax.axis_size("dp") * lax.axis_size("expert")
    experts = pieces // 2
    tok_count, feat_width = tokens.shape
    mine = (lax.axis_index("dp") * lax.axis_size("expert") + lax.axis_index("expert")) // 2
    onehot = expert_ids[:, :, None] == jnp.arange(experts, dtype=jnp.int32)
    table = jnp.sum(jnp.where(onehot, route_weight[:, :, None], 0.0), axis=1)
    both = lax.all_gather(jnp.concatenate([tokens, out_grad], axis=1), AXES, axis=0, tiled=True)
    x_all, g_all = (both[:, :feat_width], both[:, feat_width:])
    weights = lax.all_gather(table, AXES, axis=0, tiled=True)
    weight = lax.dynamic_slice_in_dim(weights, mine, 1, 1)
    w_gate, w_up, w_down = (gate_weight[0], up_weight[0], down_weight[0])
    gate_act = contract(x_all, w_gate, 1, 0)
    up_act = contract(x_all, w_up, 1, 0)
    back = contract(g_all, w_down, 1, 1)
    sig = jax.nn.sigmoid(gate_act)
    hidden = gate_act * sig * up_act
    route = jnp.sum(hidden * back, axis=1)
    scaled_hidden = (weight * hidden).astype(jnp.bfloat16)
    back = weight * back
    gate_pre = (back * up_act * sig * (1.0 + gate_act * (1.0 - sig))).astype(jnp.bfloat16)
    up_pre = (back * gate_act * sig).astype(jnp.bfloat16)
    out_part = contract(scaled_hidden, w_down, 1, 0).astype(jnp.bfloat16)
    grad_part = (contract(gate_pre, w_gate, 1, 1) + contract(up_pre, w_up, 1, 1)).astype(
        jnp.bfloat16
    )
    gate_grad = contract(x_all, gate_pre, 0, 0).astype(jnp.bfloat16)
    up_grad = contract(x_all, up_pre, 0, 0).astype(jnp.bfloat16)
    down_grad = contract(scaled_hidden, g_all, 0, 0).astype(jnp.bfloat16)
    summed = lax.psum_scatter(
        jnp.concatenate([out_part, grad_part], axis=1), AXES, scatter_dimension=0, tiled=True
    )
    routes = lax.all_to_all(route.reshape(pieces, tok_count), AXES, 0, 0, tiled=True)
    routes = jnp.sum(routes.reshape(experts, 2, tok_count), axis=1)
    route_grad = jnp.sum(jnp.where(onehot, routes.T[:, None, :], 0.0), axis=2)
    return (
        summed[:, :feat_width],
        summed[:, feat_width:],
        route_grad,
        gate_grad[None],
        up_grad[None],
        down_grad[None],
    )


def body(tokens, expert_ids, route_weight, out_grad, gate_weight, up_weight, down_weight):
    dp_size = lax.axis_size("dp")
    ex_size = lax.axis_size("expert")
    tok_count, feat_width = tokens.shape
    top_count = expert_ids.shape[1]
    experts = dp_size * ex_size // 2
    assigned = tok_count * top_count
    capacity = 2 * (assigned // experts)
    half_index = lax.axis_index("expert") % 2
    flat_ids = expert_ids.reshape(-1)
    onehot = (flat_ids[:, None] == jnp.arange(experts, dtype=jnp.int32)[None, :]).astype(jnp.int32)
    before = jnp.cumsum(onehot, axis=0) - onehot
    slot_ids = jnp.sum(before * onehot, axis=1)
    place_row = flat_ids * capacity + slot_ids
    source = (
        jnp.full((experts * capacity,), -1, jnp.int32)
        .at[place_row]
        .set(jnp.arange(assigned, dtype=jnp.int32))
    )
    filled = source >= 0
    assign = jnp.maximum(source, 0)
    rows_tok = assign // top_count
    send_rows = jnp.where(filled[:, None], tokens[rows_tok], jnp.zeros((), jnp.bfloat16))
    in_rows = deliver(send_rows, dp_size, ex_size, experts, capacity, False)
    w_gate = gate_weight[0]
    w_up = up_weight[0]
    w_down = down_weight[0]
    gate_act = jnp.dot(in_rows, w_gate, preferred_element_type=jnp.float32)
    up_act = jnp.dot(in_rows, w_up, preferred_element_type=jnp.float32)
    sig_gate = jax.nn.sigmoid(gate_act)
    hidden = (gate_act * sig_gate * up_act).astype(jnp.bfloat16)
    partial_value = jnp.dot(hidden, w_down, preferred_element_type=jnp.float32).astype(jnp.bfloat16)
    expert_table = bring_back(partial_value, dp_size, ex_size, experts, capacity, half_index, False)
    expert_rows = expert_table[place_row].reshape(tok_count, top_count, feat_width)
    layer_out = jnp.sum(route_weight[:, :, None] * expert_rows.astype(jnp.float32), axis=1).astype(
        jnp.bfloat16
    )
    route_grad = jnp.einsum("tkd,td->tk", expert_rows, out_grad, preferred_element_type=jnp.float32)
    scaled = (route_weight[:, :, None] * out_grad[:, None, :].astype(jnp.float32)).astype(
        jnp.bfloat16
    )
    scaled = scaled.reshape(assigned, feat_width)
    send_grad = jnp.where(filled[:, None], scaled[assign], jnp.zeros((), jnp.bfloat16))
    grad_rows = deliver(send_grad, dp_size, ex_size, experts, capacity, True)
    hidden_grad = contract(grad_rows, w_down, 1, 1)
    gate_pre = (hidden_grad * up_act * sig_gate * (1.0 + gate_act * (1.0 - sig_gate))).astype(
        jnp.bfloat16
    )
    up_pre = (hidden_grad * gate_act * sig_gate).astype(jnp.bfloat16)
    partial_grad = (contract(gate_pre, w_gate, 1, 1) + contract(up_pre, w_up, 1, 1)).astype(
        jnp.bfloat16
    )
    gate_grad = contract(in_rows, gate_pre, 0, 0).astype(jnp.bfloat16)
    up_grad = contract(in_rows, up_pre, 0, 0).astype(jnp.bfloat16)
    down_grad = contract(hidden, grad_rows, 0, 0).astype(jnp.bfloat16)
    grad_table = bring_back(partial_grad, dp_size, ex_size, experts, capacity, half_index, True)
    expert_grad = grad_table[place_row].reshape(tok_count, top_count, feat_width)
    token_grad = jnp.sum(expert_grad.astype(jnp.float32), axis=1).astype(jnp.bfloat16)
    return (layer_out, token_grad, route_grad, gate_grad[None], up_grad[None], down_grad[None])


def solution(mesh):
    in_specs = (
        P(("dp", "expert"), None),
        P(("dp", "expert"), None),
        P(("dp", "expert"), None),
        P(("dp", "expert"), None),
        P(("dp", "expert"), None, None),
        P(("dp", "expert"), None, None),
        P(("dp", "expert"), None, None),
    )
    out_specs = (
        P(("dp", "expert"), None),
        P(("dp", "expert"), None),
        P(("dp", "expert"), None),
        P(("dp", "expert"), None, None),
        P(("dp", "expert"), None, None),
        P(("dp", "expert"), None, None),
    )
    pieces = mesh.shape["dp"] * mesh.shape["expert"]

    def step(tokens, expert_ids, *rest):
        capacity = 2 * (tokens.shape[0] * expert_ids.shape[1] // (pieces // 2))
        form = dense_body if capacity >= tokens.shape[0] else body
        return form(tokens, expert_ids, *rest)

    return jax.shard_map(step, mesh=mesh, in_specs=in_specs, out_specs=out_specs, check_vma=False)
```

profile of v0, /device:TPU:0, one launch (start us, length us, event | category | flops | bytes accessed | tf_op | source)
XLA Modules:
  0.0 291.6 jit_solution(5355917034021186230)
XLA Ops:
  7.2 0.0 copy-start
  7.2 0.0 all-gather.2.cloned.1.call-start
  7.2 1.6 pad_maximum_fusion.1
  8.9 0.0 all-gather.2.cloned.1.call-update
  8.9 0.0 copy-start.1
  8.9 67.0 %all-gather.2.cloned.1.call-done = bf16[512,4096]{1,0:T(8,128)(2,1)} async-done(((bf16[16,4096]{1,0:T(8,128)(2,1)}), bf16[512,4096]{1,0:T(8,128)(2,1)}) %all-gather.2.cloned.1.call-update) | async-done | bytes 4194320 | tf_op jit(solution)/shard_map/all_gather | solution.py:84
  75.9 3.1 %fusion.9 = f32[512,384]{0,1:T(8,128)S(1)} fusion(bf16[1,2048,384]{2,1,0:T(8,128)(2,1)} %param.12, bf16[512,4096]{1,0:T(8,128)(2,1)} %all-gather.2.cloned.1.call-done), kind=kOutput, calls=%fused_computation.15 | convolution fusion | flops 805306368 | bytes 4456448 | tf_op jit(solution)/shard_map/dot_general | solution.py:12
  79.0 0.0 copy-done.1
  79.0 0.0 copy-start.4
  79.0 0.0 copy-start.12
  79.0 2.9 %fusion.13 = f32[512,384]{0,1:T(8,128)S(1)} fusion(bf16[1,2048,384]{2,1,0:T(8,128)(2,1)S(1)} %copy-done.1, bf16[512,4096]{1,0:T(8,128)(2,1)} %all-gather.2.cloned.1.call-done), kind=kOutput, calls=%fused_computation.19 | convolution fusion | flops 805306368 | bytes 4456448 | tf_op jit(solution)/shard_map/dot_general | solution.py:12
  82.0 0.0 copy-done.4
  82.0 0.0 copy-done
  82.0 0.1 copy-done.12
  82.1 1.9 multiply_reduce_fusion
  84.1 0.0 copy-done.6
  84.1 0.7 all_to_all.6
  84.7 3.4 %all-to-all-start = ((f32[32,1,16]{2,1,0:T(1,128)}), f32[32,1,16]{2,1,0:T(1,128)S(1)}, u32[]{:S(2)}, u32[]{:S(2)}) async-start(f32[32,1,16]{2,1,0:T(1,128)} %bitcast.3), calls=%async_computation.1 | async-start | bytes 32768 | tf_op jit(solution)/shard_map/all_to_all | solution.py:109
  88.1 0.0 reduce-scatter.2.cloned.1.call-start
  88.2 0.0 copy-done.10
  88.2 0.1 copy.21
  88.3 0.0 copy-done.11
  88.3 0.1 copy.22
  88.4 6.9 %all-to-all-done = f32[32,1,16]{2,1,0:T(1,128)S(1)} async-done(((f32[32,1,16]{2,1,0:T(1,128)}), f32[32,1,16]{2,1,0:T(1,128)S(1)}, u32[]{:S(2)}, u32[]{:S(2)}) %all-to-all-start) | async-done | bytes 2080 | tf_op jit(solution)/shard_map/all_to_all | solution.py:109
  95.3 0.1 copy.24
  95.3 0.2 select_reduce_fusion
  95.5 37.6 %all_gather.6 = f32[512,16]{1,0:T(8,128)S(1)} all-gather(f32[16,16]{1,0:T(8,128)S(1)} %get-tuple-element.13), channel_id=1, replica_groups=mesh['dp'=8,'expert'=4] {'dp','expert'}, dimensions={0}, use_global_device_ids=true | all-gather | bytes 33792 | tf_op jit(solution)/shard_map/all_gather | solution.py:86
  133.1 0.2 dynamic-slice_reduce_fusion
  133.3 0.0 copy-start.5
  133.3 0.0 copy-start.7
  133.3 0.0 copy-start.9
  133.3 2.9 convolution_convert_fusion
  136.2 0.0 copy-start.2
  136.2 0.0 copy-done.5
  136.2 0.0 copy-done.7
  136.2 0.4 multiply_convert_fusion
  136.7 1.0 copy-done.2
  137.6 1.3 fusion.11
  138.9 0.1 copy-done.3
  139.0 1.4 add_convert_fusion
  140.4 2.5 pad_maximum_fusion
  142.9 0.0 reduce-scatter.2.cloned.1.call-update
  142.9 0.7 copy.25
  143.6 4.2 %fusion.1 = bf16[1,2048,384]{2,1,0:T(8,128)(2,1)} fusion(bf16[512,384]{0,1:T(8,128)(2,1)S(1)} %get-tuple-element.14, bf16[512,4096]{1,0:T(8,128)(2,1)} %all-gather.2.cloned.1.call-done), kind=kOutput, calls=%fused_computation.7 | convolution fusion | flops 806092800 | bytes 4063232 | tf_op jit(solution)/shard_map/dot_general | solution.py:12
  147.8 2.5 fusion
  150.2 2.2 fusion.2
  152.4 130.9 %reduce-scatter.2.cloned.1.call-done = bf16[16,4096]{1,0:T(8,128)(2,1)} async-done(((bf16[512,4096]{1,0:T(8,128)(2,1)}), bf16[16,4096]{1,0:T(8,128)(2,1)}) %reduce-scatter.2.cloned.1.call-update) | async-done | bytes 131088 | tf_op jit(solution)/shard_map/reduce_scatter | solution.py:106
  283.2 1.5 fusion.19
  (10 shorter events, 0.0 us)
Async XLA Ops:
  7.2 74.8 %copy-start = (bf16[1,384,2048]{2,1,0:T(8,128)(2,1)S(1)}, bf16[1,384,2048]{2,1,0:T(8,128)(2,1)}, u32[]{:S(2)}) copy-start(bf16[1,384,2048]{2,1,0:T(8,128)(2,1)} %param.13) | copy-start | bytes 4718596
  7.2 68.7 %all-gather.2.cloned.1.call-start = ((), (), s32[]{:S(2)}) async-start(), calls=%async_computation.2 | async-start | bytes 4325376 | tf_op jit(solution)/shard_map/all_gather | solution.py:84
  8.9 70.1 %copy-start.1 = (bf16[1,2048,384]{2,1,0:T(8,128)(2,1)S(1)}, bf16[1,2048,384]{2,1,0:T(8,128)(2,1)}, u32[]{:S(2)}) copy-start(bf16[1,2048,384]{2,1,0:T(8,128)(2,1)} %param.11) | copy-start | bytes 4718596
  79.0 3.0 %copy-start.4 = (f32[512,384]{0,1:T(8,128)}, f32[512,384]{0,1:T(8,128)S(1)}, u32[]{:S(2)}) copy-start(f32[512,384]{0,1:T(8,128)S(1)} %fusion.9) | copy-start | bytes 2359300
  79.0 3.1 %copy-start.12 = (bf16[512,4096]{1,0:T(8,128)(2,1)S(1)}, bf16[512,4096]{1,0:T(8,128)(2,1)}, u32[]{:S(2)}) copy-start(bf16[512,4096]{1,0:T(8,128)(2,1)} %all-gather.2.cloned.1.call-done) | copy-start | bytes 12582916
  82.1 2.0 copy-start.6
  82.1 6.1 %copy-start.10 = (s32[16,8]{0,1:T(8,128)S(1)}, s32[16,8]{0,1:T(8,128)}, u32[]{:S(2)}) copy-start(s32[16,8]{0,1:T(8,128)} %param.8) | copy-start | bytes 1540
  82.1 6.2 %copy-start.11 = (f32[16,8]{0,1:T(8,128)S(1)}, f32[16,8]{0,1:T(8,128)}, u32[]{:S(2)}) copy-start(f32[16,8]{0,1:T(8,128)} %param.9) | copy-start | bytes 1540
  84.7 10.5 %all-to-all-start = ((f32[32,1,16]{2,1,0:T(1,128)}), f32[32,1,16]{2,1,0:T(1,128)S(1)}, u32[]{:S(2)}, u32[]{:S(2)}) async-start(f32[32,1,16]{2,1,0:T(1,128)} %bitcast.3), calls=%async_computation.1 | async-start | bytes 32768 | tf_op jit(solution)/shard_map/all_to_all | solution.py:109
  88.1 195.1 %reduce-scatter.2.cloned.1.call-start = ((), (), s32[]{:S(2)}) async-start(), calls=%async_computation.3 | async-start | bytes 4325376 | tf_op jit(solution)/shard_map/reduce_scatter | solution.py:106
  133.3 2.9 %copy-start.5 = (f32[512,384]{0,1:T(8,128)S(1)}, f32[512,384]{0,1:T(8,128)}, u32[]{:S(2)}) copy-start(f32[512,384]{0,1:T(8,128)} %copy-done.4) | copy-start | bytes 2359300
  133.3 2.9 %copy-start.7 = (f32[512,384]{0,1:T(8,128)S(1)}, f32[512,384]{0,1:T(8,128)}, u32[]{:S(2)}) copy-start(f32[512,384]{0,1:T(8,128)} %copy-done.6) | copy-start | bytes 2359300
  133.3 2.9 %copy-start.9 = (f32[512,384]{0,1:T(8,128)S(1)}, f32[512,384]{0,1:T(8,128)}, u32[]{:S(2)}) copy-start(f32[512,384]{0,1:T(8,128)} %get-tuple-element.19) | copy-start | bytes 2359300
  136.2 1.4 copy-start.2
  137.6 1.4 copy-start.3
  143.6 4.2 %copy-start.13 = (bf16[512,4096]{1,0:T(8,128)(2,1)S(1)}, bf16[512,4096]{1,0:T(8,128)(2,1)}, u32[]{:S(2)}) copy-start(bf16[512,4096]{1,0:T(8,128)(2,1)} %all-gather.2.cloned.1.call-done) | copy-start | bytes 12582916
  147.7 2.5 copy-start.8
Sparse Core Ops, SparseCore 0:
  11.4 64.4 all-gather.1
  143.0 140.1 reduce-scatter.1
where the time goes:
time: 292 us
  waiting for transfers between devices  205 us (70%)
  blocking collectives  37.6 us (13%)
  matrix products  22.3 us (8%)
  between operations  14.2 us (5%)
  other arithmetic  4.72 us (2%)
  local copies, waits for them, and re-layouts  4.57 us (2%)
  starting transfers between devices  3.46 us (1%)
    reduce_scatter x1, waiting for transfers between devices, dense_body(): lax.psum_scatter(jnp.concatenate([out_part, grad_part], axis=1), AXES, sc...  131 us
    all_gather x1, waiting for transfers between devices, dense_body(): lax.all_gather(jnp.concatenate([tokens, out_grad], axis=1), AXES, axis=0,...  67 us
    all_gather x1, blocking collectives, dense_body(): weights = lax.all_gather(table, AXES, axis=0, tiled=True)  37.6 us
    dot_general x9, matrix products, contract(): lax.dot_general(left_op, right_op, (((left_dim,), (right_dim,)), ((), ())...  22.3 us
    all_to_all x1, waiting for transfers between devices, dense_body(): lax.all_to_all(route.reshape(pieces, tok_count), AXES, 0, 0, tiled=True)  6.88 us
  transfers between devices with their start and end apart: 3, of which 3 were waited for; matrix products, arithmetic and copies ran while one was open for 3% of the time, Pallas kernels for 0%

commit v1 on v0

--- a/solution.py
+++ b/solution.py
@@ -81,7 +81,16 @@
     mine = (lax.axis_index("dp") * lax.axis_size("expert") + lax.axis_index("expert")) // 2
     onehot = expert_ids[:, :, None] == jnp.arange(experts, dtype=jnp.int32)
     table = jnp.sum(jnp.where(onehot, route_weight[:, :, None], 0.0), axis=1)
-    both = lax.all_gather(jnp.concatenate([tokens, out_grad], axis=1), AXES, axis=0, tiled=True)
+    array = jnp.concatenate([tokens, out_grad], axis=1)
+    ways, here = (lax.axis_size(AXES), lax.axis_index(AXES))
+    grown, reach = (array, 1)
+    while reach < ways:
+        theirs = lax.ppermute(grown, AXES, [(d, d ^ reach) for d in range(ways)])
+        mine_first = jnp.concatenate([grown, theirs], axis=0)
+        theirs_first = jnp.concatenate([theirs, grown], axis=0)
+        grown = jnp.where(here & reach == 0, mine_first, theirs_first)
+        reach = 2 * reach
+    both = grown
     x_all, g_all = (both[:, :feat_width], both[:, feat_width:])
     weights = lax.all_gather(table, AXES, axis=0, tiled=True)
     weight = lax.dynamic_slice_in_dim(weights, mine, 1, 1)

time: 292 us -> 373 us (1.28)
  waiting for transfers between devices: 205 us -> 269 us
  starting transfers between devices: 3.46 us -> 14.3 us
  other arithmetic: 4.72 us -> 13.9 us
  matrix products: 22.3 us -> 16.9 us
    ppermute x0 -> x5, waiting for transfers between devices: none -> 131 us  [dense_body(): theirs = lax.ppermute(grown, AXES, [(d, d ^ reach) for d in range(ways)])]
    all_gather x1 -> x0, waiting for transfers between devices: 67 us -> none  [dense_body(): lax.all_gather(jnp.concatenate([tokens, out_grad], axis=1), AXES, axis=0,...]
    select_n x0 -> x5, other arithmetic: none -> 9.62 us  [dense_body(): grown = jnp.where(here & reach == 0, mine_first, theirs_first)]
    ppermute x0 -> x5, starting transfers between devices: none -> 9.12 us  [dense_body(): theirs = lax.ppermute(grown, AXES, [(d, d ^ reach) for d in range(ways)])]
    dot_general x9, matrix products: 22.3 us -> 16.9 us  [contract(): lax.dot_general(left_op, right_op, (((left_dim,), (right_dim,)), ((), ())...]
  transfers between devices with their start and end apart: 3 -> 7, of which waited for: 3 -> 7; matrix products, arithmetic and copies ran while one was open for 3% -> 3% of each run, Pallas kernels for 0% -> 0%
where the time goes in v1:
time: 373 us; the launch traced here: 372 us
  waiting for transfers between devices  269 us (72%)
  blocking collectives  37.7 us (10%)
  matrix products  16.9 us (5%)
  starting transfers between devices  14.3 us (4%)
  between operations  14.3 us (4%)
  other arithmetic  13.9 us (4%)
  local copies, waits for them, and re-layouts  6.81 us (2%)
    ppermute x5, waiting for transfers between devices, dense_body(): theirs = lax.ppermute(grown, AXES, [(d, d ^ reach) for d in range(ways)])  131 us
    reduce_scatter x1, waiting for transfers between devices, dense_body(): lax.psum_scatter(jnp.concatenate([out_part, grad_part], axis=1), AXES, sc...  131 us
    all_gather x1, blocking collectives, dense_body(): weights = lax.all_gather(table, AXES, axis=0, tiled=True)  37.7 us
    dot_general x9, matrix products, contract(): lax.dot_general(left_op, right_op, (((left_dim,), (right_dim,)), ((), ())...  16.9 us
    select_n x5, other arithmetic, dense_body(): grown = jnp.where(here & reach == 0, mine_first, theirs_first)  9.62 us
    ppermute x5, starting transfers between devices, dense_body(): theirs = lax.ppermute(grown, AXES, [(d, d ^ reach) for d in range(ways)])  9.12 us
  transfers between devices with their start and end apart: 7, of which 7 were waited for; matrix products, arithmetic and copies ran while one was open for 3% of the time, Pallas kernels for 0%

profile of v1, /device:TPU:0, one launch (start us, length us, event | category | flops | bytes accessed | tf_op | source)
XLA Modules:
  0.0 372.5 jit_solution(2702397746347863197)
XLA Ops:
  7.2 0.0 copy-start
  7.2 1.0 constant_dynamic-update-slice_fusion.1
  8.1 0.8 constant_dynamic-update-slice_fusion
  9.0 0.5 collective-permute-start
  9.5 1.0 collective-permute-done
  10.5 2.9 collective-permute-start.1
  13.4 6.6 %collective-permute-done.1 = bf16[32,4096]{1,0:T(8,128)(2,1)S(1)} collective-permute-done((bf16[32,4096]{1,0:T(8,128)(2,1)S(1)}, bf16[32,4096]{1,0:T(8,128)(2,1)S(1)}, u32[]{:S(2)}, u32[]{:S(2)}) %collective-permute-start.1) | collective-permute-done | bytes 262176 | tf_op jit(solution)/shard_map/ppermute | solution.py:88
  20.0 0.1 maximum_select_fusion.3
  20.1 1.8 collective-permute-start.2
  22.0 11.7 %collective-permute-done.2 = bf16[64,4096]{1,0:T(8,128)(2,1)} collective-permute-done((bf16[64,4096]{1,0:T(8,128)(2,1)S(1)}, bf16[64,4096]{1,0:T(8,128)(2,1)}, u32[]{:S(2)}, u32[]{:S(2)}) %collective-permute-start.2) | collective-permute-done | bytes 524320 | tf_op jit(solution)/shard_map/ppermute | solution.py:88
  33.7 1.5 maximum_select_fusion.2
  35.2 1.6 collective-permute-start.3
  36.8 22.3 %collective-permute-done.3 = bf16[128,4096]{1,0:T(8,128)(2,1)} collective-permute-done((bf16[128,4096]{1,0:T(8,128)(2,1)S(1)}, bf16[128,4096]{1,0:T(8,128)(2,1)}, u32[]{:S(2)}, u32[]{:S(2)}) %collective-permute-start.3) | collective-permute-done | bytes 1048608 | tf_op jit(solution)/shard_map/ppermute | solution.py:88
  59.1 3.6 maximum_select_fusion.1
  62.7 2.3 collective-permute-start.4
  65.0 89.3 %collective-permute-done.4 = bf16[256,4096]{1,0:T(8,128)(2,1)} collective-permute-done((bf16[256,4096]{1,0:T(8,128)(2,1)}, bf16[256,4096]{1,0:T(8,128)(2,1)}, u32[]{:S(2)}, u32[]{:S(2)}) %collective-permute-start.4) | collective-permute-done | bytes 2097184 | tf_op jit(solution)/shard_map/ppermute | solution.py:88
  154.3 4.4 %maximum_select_fusion = bf16[512,4096]{1,0:T(8,128)(2,1)S(1)} fusion(bf16[256,4096]{1,0:T(8,128)(2,1)} %collective-permute-done.4, bf16[256,4096]{1,0:T(8,128)(2,1)} %maximum_select_fusion.1, pred[]{:T(512)S(6)} %eq.31), kind=kLoop, calls=%fused_computation | loop fusion | flops 18874368 | bytes 8388609 | tf_op jit(solution)/shard_map/jit(_where)/select_n | solution.py:91
  158.7 0.0 copy-start.3
  158.7 1.0 fusion.9
  159.8 1.5 copy-done.3
  161.3 1.0 fusion.13
  162.4 0.0 copy-start.7
  162.4 2.0 multiply_reduce_fusion
  164.4 0.7 all_to_all.6
  165.1 5.1 %all-to-all-start = ((f32[32,1,16]{2,1,0:T(1,128)}), f32[32,1,16]{2,1,0:T(1,128)S(1)}, u32[]{:S(2)}, u32[]{:S(2)}) async-start(f32[32,1,16]{2,1,0:T(1,128)} %bitcast.3), calls=%async_computation.1 | async-start | bytes 32768 | tf_op jit(solution)/shard_map/all_to_all | solution.py:118
  170.3 0.0 reduce-scatter.2.cloned.1.call-start
  170.3 0.1 copy.21
  170.4 0.1 copy.22
  170.5 6.9 %all-to-all-done = f32[32,1,16]{2,1,0:T(1,128)S(1)} async-done(((f32[32,1,16]{2,1,0:T(1,128)}), f32[32,1,16]{2,1,0:T(1,128)S(1)}, u32[]{:S(2)}, u32[]{:S(2)}) %all-to-all-start) | async-done | bytes 2080 | tf_op jit(solution)/shard_map/all_to_all | solution.py:118
  177.4 0.1 copy.24
  177.5 0.2 select_reduce_fusion
  177.6 37.7 %all_gather.3 = f32[512,16]{1,0:T(8,128)S(1)} all-gather(f32[16,16]{1,0:T(8,128)S(1)} %get-tuple-element.13), channel_id=1, replica_groups=mesh['dp'=8,'expert'=4] {'dp','expert'}, dimensions={0}, use_global_device_ids=true | all-gather | bytes 33792 | tf_op jit(solution)/shard_map/all_gather | solution.py:95
  215.4 0.2 dynamic-slice_reduce_fusion
  215.6 0.0 copy-start.9
  215.6 1.3 convolution_convert_fusion
  217.0 1.6 multiply_convert_fusion
  218.6 0.0 copy-start.6
  218.6 1.3 fusion.11
  220.0 0.1 copy-done.6
  220.0 1.4 add_convert_fusion
  221.4 2.4 pad_maximum_fusion
  223.8 0.0 reduce-scatter.2.cloned.1.call-update
  223.9 0.7 copy.25
  224.5 4.2 %fusion.1 = bf16[1,2048,384]{2,1,0:T(8,128)(2,1)} fusion(bf16[512,384]{0,1:T(8,128)(2,1)S(1)} %get-tuple-element.14, bf16[512,4096]{1,0:T(8,128)(2,1)} %copy-done.1), kind=kOutput, calls=%fused_computation.8 | convolution fusion | flops 806092800 | bytes 4063232 | tf_op jit(solution)/shard_map/dot_general | solution.py:12
  228.7 2.5 fusion
  231.2 2.2 fusion.2
  233.4 130.7 %reduce-scatter.2.cloned.1.call-done = bf16[16,4096]{1,0:T(8,128)(2,1)} async-done(((bf16[512,4096]{1,0:T(8,128)(2,1)}), bf16[16,4096]{1,0:T(8,128)(2,1)}) %reduce-scatter.2.cloned.1.call-update) | async-done | bytes 131088 | tf_op jit(solution)/shard_map/reduce_scatter | solution.py:115
  364.1 1.5 fusion.19
  (19 shorter events, 0.1 us)
Async XLA Ops:
  7.2 155.2 %copy-start = (bf16[1,384,2048]{2,1,0:T(8,128)(2,1)S(1)}, bf16[1,384,2048]{2,1,0:T(8,128)(2,1)}, u32[]{:S(2)}) copy-start(bf16[1,384,2048]{2,1,0:T(8,128)(2,1)} %param.13) | copy-start | bytes 4718596
  9.0 1.5 collective-permute-start
  10.5 9.5 %collective-permute-start.1 = (bf16[32,4096]{1,0:T(8,128)(2,1)S(1)}, bf16[32,4096]{1,0:T(8,128)(2,1)S(1)}, u32[]{:S(2)}, u32[]{:S(2)}) collective-permute-start(bf16[32,4096]{1,0:T(8,128)(2,1)S(1)} %maximum_select_fusion.4), channel_id=1, source_target_pairs={{0,2},{1,3},{2,0},{3,1},{4,6},{5,7},{6,4},{7,5},{8,10},{9,11},{10,... | collective-permute-start | bytes 786440 | tf_op jit(solution)/shard_map/ppermute | solution.py:88
  20.1 13.6 %collective-permute-start.2 = (bf16[64,4096]{1,0:T(8,128)(2,1)S(1)}, bf16[64,4096]{1,0:T(8,128)(2,1)}, u32[]{:S(2)}, u32[]{:S(2)}) collective-permute-start(bf16[64,4096]{1,0:T(8,128)(2,1)S(1)} %maximum_select_fusion.3), channel_id=1, source_target_pairs={{0,4},{1,5},{2,6},{3,7},{4,0},{5,1},{6,2},{7,3},{8,12},{9,13},{10,... | collective-permute-start | bytes 1572872 | tf_op jit(solution)/shard_map/ppermute | solution.py:88
  35.2 24.0 %collective-permute-start.3 = (bf16[128,4096]{1,0:T(8,128)(2,1)S(1)}, bf16[128,4096]{1,0:T(8,128)(2,1)}, u32[]{:S(2)}, u32[]{:S(2)}) collective-permute-start(bf16[128,4096]{1,0:T(8,128)(2,1)S(1)} %maximum_select_fusion.2), channel_id=1, source_target_pairs={{0,8},{1,9},{2,10},{3,11},{4,12},{5,13},{6,14},{7,15},{8,0},{9,1},... | collective-permute-start | bytes 3145736 | tf_op jit(solution)/shard_map/ppermute | solution.py:88
  62.7 91.6 %collective-permute-start.4 = (bf16[256,4096]{1,0:T(8,128)(2,1)}, bf16[256,4096]{1,0:T(8,128)(2,1)}, u32[]{:S(2)}, u32[]{:S(2)}) collective-permute-start(bf16[256,4096]{1,0:T(8,128)(2,1)} %maximum_select_fusion.1), channel_id=1, source_target_pairs={{0,16},{1,17},{2,18},{3,19},{4,20},{5,21},{6,22},{7,23},{8,24},{9,... | collective-permute-start | bytes 6291464 | tf_op jit(solution)/shard_map/ppermute | solution.py:88
  65.0 93.7 %copy-start.5 = (bf16[1,2048,384]{2,1,0:T(8,128)(2,1)S(1)}, bf16[1,2048,384]{2,1,0:T(8,128)(2,1)}, u32[]{:S(2)}) copy-start(bf16[1,2048,384]{2,1,0:T(8,128)(2,1)} %param.12) | copy-start | bytes 4718596
  158.7 3.6 copy-start.1
  158.7 2.6 copy-start.3
  162.4 53.2 %copy-start.7 = (f32[512,384]{0,1:T(8,128)}, f32[512,384]{0,1:T(8,128)S(1)}, u32[]{:S(2)}) copy-start(f32[512,384]{0,1:T(8,128)S(1)} %fusion.13) | copy-start | bytes 2359300
  162.4 7.9 %copy-start.10 = (s32[16,8]{0,1:T(8,128)S(1)}, s32[16,8]{0,1:T(8,128)}, u32[]{:S(2)}) copy-start(s32[16,8]{0,1:T(8,128)} %param.8) | copy-start | bytes 1540
  162.4 8.0 %copy-start.11 = (f32[16,8]{0,1:T(8,128)S(1)}, f32[16,8]{0,1:T(8,128)}, u32[]{:S(2)}) copy-start(f32[16,8]{0,1:T(8,128)} %param.9) | copy-start | bytes 1540
  165.1 12.3 %all-to-all-start = ((f32[32,1,16]{2,1,0:T(1,128)}), f32[32,1,16]{2,1,0:T(1,128)S(1)}, u32[]{:S(2)}, u32[]{:S(2)}) async-start(f32[32,1,16]{2,1,0:T(1,128)} %bitcast.3), calls=%async_computation.1 | async-start | bytes 32768 | tf_op jit(solution)/shard_map/all_to_all | solution.py:118
  170.3 193.8 %reduce-scatter.2.cloned.1.call-start = ((), (), s32[]{:S(2)}) async-start(), calls=%async_computation.2 | async-start | bytes 4325376 | tf_op jit(solution)/shard_map/reduce_scatter | solution.py:115
  215.6 1.4 copy-start.9
  217.0 1.7 copy-start.4
  218.6 1.4 copy-start.6
  224.5 4.2 %copy-start.2 = (bf16[512,4096]{1,0:T(8,128)(2,1)S(1)}, bf16[512,4096]{1,0:T(8,128)(2,1)}, u32[]{:S(2)}) copy-start(bf16[512,4096]{1,0:T(8,128)(2,1)} %copy-done.1) | copy-start | bytes 12582916
  228.7 2.5 copy-start.8
Sparse Core Ops, SparseCore 0:
  224.0 140.0 reduce-scatter.1
